TPU v7x, 32 devices: a whole 2x2x4 slice. The times are simulated.
32 devices in a mesh: group: 8 (over z, x), sub: 4 (over y, core).
Axes of the slice: x: 2, y: 2, z: 4, core: 2. Of those that a mesh axis runs over, the one named last changes fastest.
Arguments:
- embeddings: bfloat16 [65536, 768], P(('group', 'sub'))
- labels: int32 [512], P(('group', 'sub')), may hold values from 0 to 1, as said below
- group_bit: int32 [1], replicated, may hold values from 0 to 2
- init_index: int32 [8, 128], P('group'), may hold values from 0 to 8191
Outputs:
- centroids: float32 [8, 128, 768], P('group')
- counts: float32 [8, 128], P('group')
Inputs may be any that keep to these rules, and one draw needn't show every extreme that they name: `labels`: each label is a child, 0 or 1. `init_index`: row numbers within group g, counted along the sub axis in order.
All inputs are finite; a program needn't handle non-finite values.
Results may differ from a plain program's by a relative error of at most 0.0031.
Values may be sent and summed in bfloat16 or wider, within the bound.
No kernel may reach another device: no remote copies, remote signals or barrier semaphores. Data moves between devices by JAX's collectives and lax.ppermute only.
A program may use at most 64 MiB of HBM per device.

v0:
```python
from functools import partial

import jax
import jax.numpy as jnp
from jax import lax
from jax.sharding import PartitionSpec as P

ITERS = 2


prior_weight = 1.0


def shortened(value):
    return jax.tree.map(lambda a: a.astype(jnp.bfloat16) if a.dtype == jnp.float32 else a, value)


def partner(value, axis, stride):
    mask = 2**stride
    pairs = [(source, source ^ mask) for source in range(lax.axis_size(axis))]
    return lax.ppermute(value, axis, pairs)


def responsibility_terms(row_vectors, retained_rows, centroids, softness_scale):
    cent_half = centroids.astype(jnp.bfloat16)
    centroid_norm_values = jnp.sum(jnp.square(cent_half.astype(jnp.float32)), axis=1)
    distance_scores = jnp.dot(row_vectors, cent_half.T, preferred_element_type=jnp.float32)
    assignment_logits = (2.0 * distance_scores - centroid_norm_values[None, :]) / softness_scale
    weights = (
        jax.nn.softmax(assignment_logits, axis=1).astype(jnp.bfloat16) * retained_rows[:, None]
    )
    weighted_totals = lax.dot_general(
        weights, row_vectors, (((0,), (0,)), ((), ())), preferred_element_type=jnp.float32
    )
    counts = jnp.sum(weights.astype(jnp.float32), axis=0)
    return (weighted_totals, counts)


def swap_pair(paired, bit_level):
    return partner((shortened(paired[0]), shortened(paired[1])), "group", bit_level)


def block_mask(marks, own_side, block_rows):
    chosen_rows = (marks == own_side).astype(jnp.bfloat16)
    return jnp.broadcast_to(chosen_rows[:, None], (marks.shape[0], block_rows)).reshape(-1)


def local(embeddings, labels, group_bit, init_index):
    rows_here = embeddings.shape[0]
    feature_width = embeddings.shape[1]
    block_rows = rows_here // labels.shape[0]
    softness_scale = feature_width / 8.0
    chosen = group_bit[0]
    own_side = jnp.bitwise_and(jnp.right_shift(lax.axis_index("group"), chosen), 1)
    levels = lax.axis_size("group").bit_length() - 1
    kept_own = block_mask(labels, own_side, block_rows)
    branches = [partial(swap_pair, bit_level=level_number) for level_number in range(levels)]
    received, their_labels = lax.switch(chosen, branches, (embeddings, labels))
    kept_their = block_mask(their_labels, own_side, block_rows)
    first_row = lax.axis_index("sub") * rows_here
    picked = init_index[0] - first_row
    onehot = (picked[:, None] == jnp.arange(rows_here, dtype=jnp.int32)[None, :]).astype(
        jnp.bfloat16
    )
    centroids = lax.psum(
        jnp.dot(onehot, embeddings, preferred_element_type=jnp.float32).astype(jnp.bfloat16), "sub"
    ).astype(jnp.float32)
    counts = jnp.zeros((centroids.shape[0],), jnp.float32)
    for iteration in range(ITERS):
        candidate_rows = jnp.concatenate([embeddings, received], axis=0)
        retained_rows = jnp.concatenate([kept_own, kept_their], axis=0)
        weighted_totals, counts = responsibility_terms(
            candidate_rows, retained_rows, centroids, softness_scale
        )
        weighted_totals, counts = lax.psum((weighted_totals, counts), "sub")
        centroids = (weighted_totals + prior_weight * centroids) / (counts[:, None] + prior_weight)
    return (centroids[None], counts[None])


def solution(mesh):
    return jax.shard_map(
        local,
        mesh=mesh,
        in_specs=(P(("group", "sub"), None), P(("group", "sub")), P(), P("group", None)),
        out_specs=(P("group", None, None), P("group", None)),
        check_vma=False,
    )
```

profile of v0, /device:TPU:0, one launch (start us, length us, event | category | flops | bytes accessed | tf_op | source)
XLA Modules:
  0.0 183.5 jit_solution(15986342576699027701)
XLA Ops:
  7.2 0.0 all-reduce.4.cloned.1.call-start
  7.2 0.8 subtract_bitcast_fusion
  8.0 3.3 %convolution_convert_fusion = bf16[128,768]{1,0:T(8,128)(2,1)} fusion(bf16[2048,768]{1,0:T(8,128)(2,1)} %param.7, s32[128]{0:T(128)S(1)} %subtract_bitcast_fusion), kind=kOutput, calls=%fused_computation.14 | convolution fusion | flops 403013632 | bytes 3342848 | tf_op jit(solution)/shard_map/dot_general | solution.py:66
  11.3 0.0 all-reduce.4.cloned.1.call-update
  11.4 0.0 all-reduce.6.cloned.1.call-start
  11.4 1.9 %constant_dynamic-update-slice_fusion.1 = bf16[4096,768]{1,0:T(8,128)(2,1)} fusion(bf16[2048,768]{1,0:T(8,128)(2,1)S(1)} %copy-done), kind=kLoop, calls=%fused_computation.28 | loop fusion | bytes 6291456
  14.0 71.4 %conditional.1 = (bf16[2048,768]{1,0:T(8,128)(2,1)}, s32[16]{0:T(128)}) conditional(s32[]{:T(128)} %clamp.3, (bf16[2048,768]{1,0:T(8,128)(2,1)S(1)}, s32[16]{0:T(128)S(1)}) %tuple.39, (bf16[2048,768]{1,0:T(8,128)(2,1)S(1)}, s32[16]{0:T(128)S(1)}) %tuple.40, (bf16[2048,768]{1,0:T(8,128)(2,1)S(1)}, s32[16]{0:T(128)S(1)}) %tuple.41), branch_computations={%region_0.0_spmd, %region_1.0_spmd, %region_2.0_spmd} | conditional | bytes 12583264 | solution.py:58
  14.0 3.1 %collective-permute-start.2 = (bf16[2048,768]{1,0:T(8,128)(2,1)S(1)}, bf16[2048,768]{1,0:T(8,128)(2,1)}, u32[]{:S(2)}, u32[]{:S(2)}) collective-permute-start(bf16[2048,768]{1,0:T(8,128)(2,1)S(1)} %get-tuple-element.14), channel_id=1, source_target_pairs={{0,8},{4,12},{8,0},{12,4},{16,24},{20,28},{24,16},{28,20},{1,9},{5... | collective-permute-start | bytes 9437192 | tf_op jit(solution)/shard_map/cond/branch_1_fun/ppermute | solution.py:21
  17.1 0.1 collective-permute-start.3
  17.1 68.2 %collective-permute-done.3 = s32[16]{0:T(128)} collective-permute-done((s32[16]{0:T(128)S(1)}, s32[16]{0:T(128)}, u32[]{:S(2)}, u32[]{:S(2)}) %collective-permute-start.3) | collective-permute-done | bytes 96 | tf_op jit(solution)/shard_map/cond/branch_1_fun/ppermute | solution.py:21
  85.3 0.6 compare_convert_fusion
  86.0 0.1 broadcast_bitcast_fusion
  86.0 0.1 broadcast_bitcast_fusion.1
  86.1 3.8 %constant_dynamic-update-slice_fusion = bf16[4096,768]{1,0:T(8,128)(2,1)} fusion(bf16[4096,768]{1,0:T(8,128)(2,1)} %constant_dynamic-update-slice_fusion.1, bf16[2048,768]{1,0:T(8,128)(2,1)} %get-tuple-element.22), kind=kLoop, calls=%fused_computation.27 | loop fusion | bytes 6291456 | tf_op jit(solution)/shard_map/concatenate | solution.py:70
  89.9 1.2 fusion.9
  91.1 5.1 %fusion.15 = (f32[4096]{0:T(1024)S(1)}, f32[4096,128]{0,1:T(8,128)S(1)}) fusion(f32[128]{0:T(128)S(1)} %fusion.9, bf16[4096,768]{1,0:T(8,128)(2,1)} %constant_dynamic-update-slice_fusion, bf16[128,768]{1,0:T(8,128)(2,1)} %all-reduce.4.cloned.1.call-done), kind=kOutput, calls=%fused_computation.36 | convolution fusion | flops 807399424 | bytes 8602112 | tf_op jit(solution)/shard_map/dot_general | solution.py:27
  96.2 0.3 fusion.4
  96.6 0.5 convert_reduce_fusion.1
  97.1 1.8 fusion.17
  98.9 0.0 all-reduce.6.cloned.1.call-update
  98.9 0.0 all-reduce.8.cloned.1.call-start
  99.0 5.8 %psum.37 = f32[128]{0:T(128)S(1)} all-reduce(f32[128]{0:T(128)S(1)} %get-tuple-element.26), channel_id=1, replica_groups=mesh['group'=8,'sub'=4] {'sub'}, use_global_device_ids=true, to_apply=%region_9.0 | all-reduce | flops 128 | bytes 1024 | tf_op jit(solution)/shard_map/psum | solution.py:75
  104.8 28.3 %all-reduce.6.cloned.1.call-done = f32[128,768]{1,0:T(8,128)} async-done(((f32[128,768]{1,0:T(8,128)}), f32[128,768]{1,0:T(8,128)}) %all-reduce.6.cloned.1.call-update) | async-done | bytes 393232 | tf_op jit(solution)/shard_map/psum | solution.py:75
  133.1 1.3 multiply_reduce_fusion
  134.5 5.1 %fusion.16 = (f32[4096]{0:T(1024)S(1)}, f32[4096,128]{0,1:T(8,128)S(1)}) fusion(f32[128]{0:T(128)S(1)} %multiply_reduce_fusion, bf16[4096,768]{1,0:T(8,128)(2,1)} %constant_dynamic-update-slice_fusion, f32[128]{0:T(128)S(1)} %broadcast_add_fusion.1, f32[128,768]{1,0:T(8,128)} %all-reduce.6.cloned.1.call-done, bf16[128,768]{1,0:T(8,128)(2,1)S(1)} %copy-done.1), kind=kOutput, calls=%fused_computation.37 | convolution fusion | flops 807792640 | bytes 8995840 | tf_op jit(solution)/shard_map/dot_general | solution.py:27
  139.6 0.3 fusion.5
  139.9 0.5 convert_reduce_fusion
  140.5 1.8 fusion.18
  142.3 0.0 all-reduce.8.cloned.1.call-update
  142.3 5.8 %psum.39 = f32[128]{0:T(128)S(1)} all-reduce(f32[128]{0:T(128)S(1)} %get-tuple-element.24), channel_id=1, replica_groups=mesh['group'=8,'sub'=4] {'sub'}, use_global_device_ids=true, to_apply=%region_15.0 | all-reduce | flops 128 | bytes 1024 | tf_op jit(solution)/shard_map/psum | solution.py:75
  148.1 27.0 %all-reduce.8.cloned.1.call-done = f32[128,768]{1,0:T(8,128)} async-done(((f32[128,768]{1,0:T(8,128)}), f32[128,768]{1,0:T(8,128)}) %all-reduce.8.cloned.1.call-update) | async-done | bytes 393232 | tf_op jit(solution)/shard_map/psum | solution.py:75
  175.1 1.9 %divide_bitcast_fusion = f32[1,128,768]{2,1,0:T(8,128)} fusion(f32[128,768]{1,0:T(8,128)} %all-reduce.8.cloned.1.call-done, f32[128]{0:T(128)S(1)} %broadcast_add_fusion, f32[128]{0:T(128)S(1)} %broadcast_add_fusion.1, f32[128,768]{1,0:T(8,128)S(1)} %copy-done.2, bf16[128,768]{1,0:T(8,128)(2,1)S(1)} %copy-done.1), kind=kLoop, calls=%fused_computation.23 | loop fusion | flops 491520 | bytes 1377280 | tf_op jit(solution)/shard_map/broadcast_in_dim | solution.py:77
  (25 shorter events, 0.1 us)
Async XLA Ops:
  7.2 4.3 %copy-start = (bf16[2048,768]{1,0:T(8,128)(2,1)S(1)}, bf16[2048,768]{1,0:T(8,128)(2,1)}, u32[]{:S(2)}) copy-start(bf16[2048,768]{1,0:T(8,128)(2,1)} %param.7) | copy-start | bytes 9437188
  7.2 82.7 %all-reduce.4.cloned.1.call-start = ((), (), s32[]{:S(2)}) async-start(), calls=%async_computation | async-start | bytes 393216 | tf_op jit(solution)/shard_map/psum | solution.py:65
  11.4 2.6 %copy-start.3 = (s32[16]{0:T(128)S(1)}, s32[16]{0:T(128)}, u32[]{:S(2)}) copy-start(s32[16]{0:T(128)} %param.8) | copy-start | bytes 196
  11.4 121.8 %all-reduce.6.cloned.1.call-start = ((), (), s32[]{:S(2)}) async-start(), calls=%async_computation.1 | async-start | bytes 786432 | tf_op jit(solution)/shard_map/psum | solution.py:75
  14.0 71.4 %collective-permute-start.2 = (bf16[2048,768]{1,0:T(8,128)(2,1)S(1)}, bf16[2048,768]{1,0:T(8,128)(2,1)}, u32[]{:S(2)}, u32[]{:S(2)}) collective-permute-start(bf16[2048,768]{1,0:T(8,128)(2,1)S(1)} %get-tuple-element.14), channel_id=1, source_target_pairs={{0,8},{4,12},{8,0},{12,4},{16,24},{20,28},{24,16},{28,20},{1,9},{5... | collective-permute-start | bytes 9437192 | tf_op jit(solution)/shard_map/cond/branch_1_fun/ppermute | solution.py:21
  17.1 68.3 %collective-permute-start.3 = (s32[16]{0:T(128)S(1)}, s32[16]{0:T(128)}, u32[]{:S(2)}, u32[]{:S(2)}) collective-permute-start(s32[16]{0:T(128)S(1)} %get-tuple-element.15), channel_id=1, source_target_pairs={{0,8},{4,12},{8,0},{12,4},{16,24},{20,28},{24,16},{28,20},{1,9},{5... | collective-permute-start | bytes 200 | tf_op jit(solution)/shard_map/cond/branch_1_fun/ppermute | solution.py:21
  89.9 7.2 %slice-start = ((s8[6291456]{0:T(1024)(128)(4,1)}), s8[4194304]{0:T(1024)(128)(4,1)S(1)}, s32[]{:S(2)}) async-start(s8[6291456]{0:T(1024)(128)(4,1)} %bitcast.20), calls=%async_computation.3 | async-start | bytes 8388608
  91.1 6.0 %slice-start.1 = ((s8[6291456]{0:T(1024)(128)(4,1)}), s8[2097152]{0:T(1024)(128)(4,1)S(1)}, s32[]{:S(2)}) async-start(s8[6291456]{0:T(1024)(128)(4,1)} %bitcast.20), calls=%async_computation.4 | async-start | bytes 4194304
  97.1 36.0 %copy-start.1 = (bf16[128,768]{1,0:T(8,128)(2,1)S(1)}, bf16[128,768]{1,0:T(8,128)(2,1)}, u32[]{:S(2)}) copy-start(bf16[128,768]{1,0:T(8,128)(2,1)} %all-reduce.4.cloned.1.call-done) | copy-start | bytes 589828
  98.9 76.2 %all-reduce.8.cloned.1.call-start = ((), (), s32[]{:S(2)}) async-start(), calls=%async_computation.2 | async-start | bytes 786432 | tf_op jit(solution)/shard_map/psum | solution.py:75
  133.1 7.4 %slice-start.2 = ((s8[6291456]{0:T(1024)(128)(4,1)}), s8[4194304]{0:T(1024)(128)(4,1)S(1)}, s32[]{:S(2)}) async-start(s8[6291456]{0:T(1024)(128)(4,1)} %bitcast.22), calls=%async_computation.5 | async-start | bytes 8388608
  134.5 6.0 %slice-start.3 = ((s8[6291456]{0:T(1024)(128)(4,1)}), s8[2097152]{0:T(1024)(128)(4,1)S(1)}, s32[]{:S(2)}) async-start(s8[6291456]{0:T(1024)(128)(4,1)} %bitcast.22), calls=%async_computation.6 | async-start | bytes 4194304
  140.5 34.6 %copy-start.2 = (f32[128,768]{1,0:T(8,128)S(1)}, f32[128,768]{1,0:T(8,128)}, u32[]{:S(2)}) copy-start(f32[128,768]{1,0:T(8,128)} %all-reduce.6.cloned.1.call-done) | copy-start | bytes 1179652
  148.1 28.9 %copy-start.4 = (f32[128]{0:T(128)}, f32[128]{0:T(128)S(1)}, u32[]{:S(2)}) copy-start(f32[128]{0:T(128)S(1)} %psum.39) | copy-start | bytes 1540
Sparse Core Ops, SparseCore 0:
  11.5 34.3 all-reduce.3
  99.1 34.0 all-reduce.5
  142.4 32.6 all-reduce.7
where the time goes:
time: 184 us
  waiting for transfers between devices  124 us (67%)
  matrix products  17.1 us (9%)
  between operations  14.6 us (8%)
  blocking collectives  11.6 us (6%)
  other arithmetic  7.56 us (4%)
  local copies, waits for them, and re-layouts  5.85 us (3%)
  starting transfers between devices  3.29 us (2%)
    ppermute x2, waiting for transfers between devices, partner(): return lax.ppermute(value, axis, pairs)  68.2 us
    psum x2, waiting for transfers between devices, local(): weighted_totals, counts = lax.psum((weighted_totals, counts), 'sub')  55.3 us
    psum x2, blocking collectives, local(): weighted_totals, counts = lax.psum((weighted_totals, counts), 'sub')  11.6 us
    dot_general x2, matrix products, responsibility_terms(): jnp.dot(row_vectors, cent_half.T, preferred_element_type=jnp.float32)  10.3 us
    concatenate x1, local copies, waits for them, and re-layouts, local(): candidate_rows = jnp.concatenate([embeddings, received], axis=0)  3.8 us
  transfers between devices with their start and end apart: 5, of which 3 were waited for; matrix products, arithmetic and copies ran while one was open for 4% of the time, Pallas kernels for 0%

commit v1 on v0

v1 whole, which is shorter than its diff:
```python
from functools import partial

import jax
import jax.numpy as jnp
from jax import lax
from jax.experimental import pallas as pl
from jax.experimental.pallas import tpu as pltpu
from jax.sharding import PartitionSpec as P

ITERS = 2
PRIOR = 1.0
CORES = 2
TAIL = 8
BF16, F32 = jnp.bfloat16, jnp.float32
AXES = ("group", "sub")
VMEM = pl.BlockSpec(memory_space=pltpu.VMEM)
SMEM = pl.BlockSpec(memory_space=pltpu.SMEM)


def contract(a, b, dim_a, dim_b):
    return lax.dot_general(a, b, (((dim_a,), (dim_b,)), ((), ())), preferred_element_type=F32)


def column(row):
    k = row.shape[1]
    diagonal = lax.broadcasted_iota(jnp.int32, (k, k), 0) == lax.broadcasted_iota(jnp.int32, (k, k), 1)
    return jnp.sum(jnp.where(diagonal, row, jnp.zeros_like(row)), axis=1, keepdims=True)


def tree(terms):
    while len(terms) > 1:
        terms = [terms[i] + terms[i + 1] for i in range(0, len(terms), 2)]
    return terms[0]


def seed_kernel(index_ref, rows_ref, out_ref):
    rows = rows_ref.shape[0]
    picked = column(index_ref[...].astype(F32)).astype(jnp.int32) - lax.axis_index("sub") * rows
    onehot = (lax.broadcasted_iota(jnp.int32, (picked.shape[0], rows), 1) == picked).astype(F32).astype(BF16)
    out_ref[...] = contract(onehot, rows_ref[...], 1, 0).astype(BF16)


def accumulate(half, centroids, own_labels, other_labels, own_rows, other_rows, out_ref, sums, counts, block, scale):
    core = lax.rem(lax.axis_index("sub"), CORES)
    k, width = centroids.shape
    square = half.astype(F32)
    norms = jnp.sum(square * square, axis=1, keepdims=True)
    rows = own_rows.shape[0]
    step = rows
    first = True
    for labels, x_ref in ((own_labels, own_rows), (other_labels, other_rows)):
        for start in range(0, rows, step):
            x = x_ref[pl.ds(start, step), :]
            logits = (2.0 * contract(half, x, 1, 1) - norms) * (1.0 / scale)
            top = jnp.max(logits, axis=0, keepdims=True)
            e = jnp.exp(logits - top)
            weights = (e * (1.0 / jnp.sum(e, axis=0, keepdims=True))).astype(BF16)
            kept = jnp.concatenate(
                [
                    jnp.full((1, block), (labels[start // block + j] == core).astype(F32))
                    for j in range(step // block)
                ],
                axis=1,
            ).astype(BF16)
            weights = weights * kept
            part = contract(weights, x, 1, 0)
            number = contract(jnp.ones((TAIL, step), BF16), weights, 1, 1)
            if first:
                sums[...] = part
                counts[...] = number
            else:
                sums[...] += part
                counts[...] += number
            first = False
    out_ref[0:k, :] = sums[...].astype(BF16)
    number = counts[...]
    high = number.astype(BF16).astype(F32)
    line = lax.broadcasted_iota(jnp.int32, number.shape, 0)
    out_ref[k : k + TAIL, :] = jnp.zeros((TAIL, width), BF16)
    out_ref[k : k + TAIL, 0:k] = jnp.where(line == 0, high, number - high).astype(BF16)


def first_kernel(bit, block, scale, n, *refs):
    own_labels, other_labels, chip_ref = refs[:3]
    parts = refs[3 : 3 + n]
    own_rows, other_rows, out_ref, c_ref, sums, counts = refs[3 + n :]
    core = lax.rem(lax.axis_index("sub"), CORES)
    side = jnp.bitwise_and(jnp.right_shift(lax.axis_index("group"), bit), 1)
    chip = chip_ref[...].astype(F32)
    centroids = jnp.where(core == side, chip, jnp.zeros_like(chip))
    for part in parts:
        centroids = centroids + part[...].astype(F32)
    half = centroids.astype(BF16)
    c_ref[...] = half
    accumulate(half, centroids, own_labels, other_labels, own_rows, other_rows, out_ref, sums, counts, block, scale)


def updated(before, parts):
    k = before.shape[0]
    total = tree([part[0:k, :].astype(F32) for part in parts])
    tails = [part[k : k + TAIL, 0:k].astype(F32) for part in parts]
    number = tree([tail[0:1, :] + tail[1:2, :] for tail in tails])
    return (total + PRIOR * before) * (1.0 / (column(number) + PRIOR)), number


def next_kernel(block, scale, n, *refs):
    own_labels, other_labels, before_ref = refs[:3]
    parts = refs[3 : 3 + n]
    own_rows, other_rows, out_ref, c_ref, sums, counts = refs[3 + n :]
    centroids, _ = updated(before_ref[...].astype(F32), [part[...] for part in parts])
    c_ref[...] = centroids
    accumulate(
        centroids.astype(BF16), centroids, own_labels, other_labels, own_rows, other_rows, out_ref, sums, counts, block,
        scale,
    )


def last_kernel(n, *refs):
    before_ref, parts, out_ref = refs[0], refs[1 : 1 + n], refs[1 + n]
    k = before_ref.shape[0]
    centroids, number = updated(before_ref[...].astype(F32), [part[...] for part in parts])
    out_ref[0:k, :] = centroids
    out_ref[k : k + TAIL, :] = jnp.zeros((TAIL, out_ref.shape[1]), F32)
    out_ref[k : k + TAIL, 0:k] = jnp.broadcast_to(number, (TAIL, k))


def call(kernel, outs, scratch=(), smem=0, vmem=0, flops=0):
    return pl.pallas_call(
        kernel,
        out_shape=outs,
        in_specs=[SMEM] * smem + [VMEM] * vmem,
        out_specs=jax.tree.map(lambda _: VMEM, outs),
        scratch_shapes=list(scratch),
        compiler_params=pltpu.CompilerParams(vmem_limit_bytes=28 << 20),
        cost_estimate=pl.CostEstimate(flops=flops, bytes_accessed=1 << 20, transcendentals=0),
    )


class Plan:
    def __init__(self, bit):
        self.mask = 1 << bit
        self.groups = lax.axis_size("group")
        self.subs = lax.axis_size("sub")
        self.chips = self.subs // CORES
        self.bit = bit

    def devices(self):
        for group in range(self.groups):
            for sub in range(self.subs):
                yield group, sub // CORES, sub % CORES, (group >> self.bit) & 1

    def flat(self, group, chip, core):
        return group * self.subs + chip * CORES + core

    def seeds(self, value):
        received = []
        for step in range(self.chips):
            pairs = []
            for group, chip, core, side in self.devices():
                source = self.flat(group, chip, core)
                if core != side:
                    pairs.append((source, self.flat(group ^ self.mask, chip ^ step, 1 - core)))
                elif step:
                    pairs.append((source, self.flat(group, chip ^ step, core)))
            received.append(lax.ppermute(value, AXES, pairs))
        return received

    def sums(self, value, last):
        received = [value]
        for flip in (0, 1):
            for step in range(self.chips):
                if not flip and not step:
                    continue
                pairs = [
                    (self.flat(group, chip, core), self.flat(group ^ (self.mask * flip), chip ^ step, core))
                    for group, chip, core, side in self.devices()
                    if not last or core == side ^ flip
                ]
                received.append(lax.ppermute(value, AXES, pairs))
        return received


def swap_cores(value):
    return lax.ppermute(value, "sub", [(sub, sub ^ 1) for sub in range(lax.axis_size("sub"))])


def refine(chip_seeds, own_labels, other_labels, own_rows, other_rows, bit):
    plan = Plan(bit)
    k, width = chip_seeds.shape
    rows = own_rows.shape[0]
    block = rows // own_labels.shape[0]
    scale = width / 8.0
    payload = jax.ShapeDtypeStruct((k + TAIL, width), BF16)
    scratch = [pltpu.VMEM((k, width), F32), pltpu.VMEM((TAIL, k), F32)]
    flops = 8 * rows * k * width

    seeds = plan.seeds(chip_seeds)
    parts, centroids = call(
        partial(first_kernel, bit, block, scale, len(seeds)),
        (payload, jax.ShapeDtypeStruct((k, width), BF16)),
        scratch, 2, 3 + len(seeds), flops,
    )(own_labels, other_labels, chip_seeds, *seeds, own_rows, other_rows)
    for _ in range(ITERS - 1):
        shares = plan.sums(parts, False)
        parts, centroids = call(
            partial(next_kernel, block, scale, len(shares)),
            (payload, jax.ShapeDtypeStruct((k, width), F32)),
            scratch, 2, 3 + len(shares), flops,
        )(own_labels, other_labels, centroids, *shares, own_rows, other_rows)
    shares = plan.sums(parts, True)
    mine = call(
        partial(last_kernel, len(shares)), jax.ShapeDtypeStruct((k + TAIL, width), F32), (), 0, 1 + len(shares)
    )(centroids, *shares)
    theirs = swap_cores(mine)
    core = lax.rem(lax.axis_index("sub"), CORES)
    side = jnp.bitwise_and(jnp.right_shift(lax.axis_index("group"), bit), 1)
    result = jnp.where(core == side, mine, theirs)
    return result[None, 0:k], result[k : k + 1, 0:k]


def local(embeddings, labels, group_bit, init_index):
    k, width = init_index.shape[1], embeddings.shape[1]
    levels = lax.axis_size("group").bit_length() - 1
    seeds = call(seed_kernel, jax.ShapeDtypeStruct((k, width), BF16), (), 0, 2)(init_index, embeddings)
    chip_seeds = seeds + swap_cores(seeds)
    other_labels = swap_cores(labels)
    other_rows = swap_cores(embeddings)
    return lax.switch(
        group_bit[0],
        [partial(refine, bit=bit) for bit in range(levels)],
        chip_seeds, labels, other_labels, embeddings, other_rows,
    )


def solution(mesh):
    return jax.shard_map(
        local,
        mesh=mesh,
        in_specs=(P(("group", "sub"), None), P(("group", "sub")), P(), P("group", None)),
        out_specs=(P("group", None, None), P("group", None)),
        check_vma=False,
    )
```

time: 184 us -> 53.8 us (0.29)
  waiting for transfers between devices: 124 us -> 22.5 us
  matrix products: 17.1 us -> 0 us
  between operations: 14.6 us -> 1.32 us
  starting transfers between devices: 3.29 us -> 14.9 us
  blocking collectives: 11.6 us -> 0 us
  Pallas kernels: 0 us -> 11 us
  other arithmetic: 7.56 us -> 0.87 us
  local copies, waits for them, and re-layouts: 5.85 us -> 2.95 us
    psum x3 -> x0, waiting for transfers between devices: 55.3 us -> none  [the longest x2 55.3 us: local(): weighted_totals, counts = lax.psum((weighted_totals, counts), 'sub')]
    ppermute x2 -> x12, waiting for transfers between devices: 68.2 us -> 22.5 us  [the longest x6 14.9 us: sums(): received.append(lax.ppermute(value, AXES, pairs))]
    dot_general x5 -> x0, matrix products: 17.1 us -> none  [the longest x2 10.3 us: responsibility_terms(): jnp.dot(row_vectors, cent_half.T, preferred_element_type=jnp.float32)]
    ppermute x2 -> x12, starting transfers between devices: 3.17 us -> 14.9 us  [the longest x6 9.9 us: sums(): received.append(lax.ppermute(value, AXES, pairs))]
    psum x2 -> x0, blocking collectives: 11.6 us -> none  [local(): weighted_totals, counts = lax.psum((weighted_totals, counts), 'sub')]
    pallas_call x0 -> x4, Pallas kernels: none -> 11 us  [the longest x1 4.11 us: refine(): call(partial(next_kernel, block, scale, len(shares)), (payload, jax.Shape...]
    reduce_sum x6 -> x0, other arithmetic: 4.25 us -> none  [the longest x2 2.54 us: responsibility_terms(): jnp.sum(jnp.square(cent_half.astype(jnp.float32)), axis=1)]
    concatenate x1 -> x0, local copies, waits for them, and re-layouts: 3.8 us -> none  [local(): candidate_rows = jnp.concatenate([embeddings, received], axis=0)]
  transfers between devices with their start and end apart: 5 -> 12, of which waited for: 3 -> 8; matrix products, arithmetic and copies ran while one was open for 4% -> 0% of each run, Pallas kernels for 0% -> 5%
where the time goes in v1:
time: 53.8 us; the launch traced here: 53.6 us
  waiting for transfers between devices  22.5 us (42%)
  starting transfers between devices  14.9 us (28%)
  Pallas kernels  11 us (20%)
  local copies, waits for them, and re-layouts  2.95 us (5%)
  between operations  1.32 us (2%)
  other arithmetic  0.87 us (2%)
    ppermute x6, waiting for transfers between devices, sums(): received.append(lax.ppermute(value, AXES, pairs))  14.9 us
    ppermute x6, starting transfers between devices, sums(): received.append(lax.ppermute(value, AXES, pairs))  9.9 us
    ppermute x2, waiting for transfers between devices, seeds(): received.append(lax.ppermute(value, AXES, pairs))  4.91 us
    pallas_call x1, Pallas kernels, refine(): call(partial(next_kernel, block, scale, len(shares)), (payload, jax.Shape...  4.11 us
    pallas_call x1, Pallas kernels, refine(): call(partial(first_kernel, bit, block, scale, len(seeds)), (payload, jax....  4.03 us
    ppermute x2, starting transfers between devices, seeds(): received.append(lax.ppermute(value, AXES, pairs))  3.79 us
    ppermute x4, waiting for transfers between devices, swap_cores(): lax.ppermute(value, 'sub', [(sub, sub ^ 1) for sub in range(lax.axis_size...  2.72 us
    pallas_call x1, Pallas kernels, local(): call(seed_kernel, jax.ShapeDtypeStruct((k, width), BF16), (), 0, 2)  2.69 us
  transfers between devices with their start and end apart: 12, of which 8 were waited for; matrix products, arithmetic and copies ran while one was open for 0% of the time, Pallas kernels for 5%

profile of v1, /device:TPU:0, one launch (start us, length us, event | category | flops | bytes accessed | tf_op | source)
XLA Modules:
  0.0 53.6 jit_solution(9954143830088766613)
XLA Ops:
  0.6 0.5 collective-permute-start.29
  1.2 0.7 %copy-done = s32[1,128]{1,0:T(1,128)S(1)} copy-done((s32[1,128]{1,0:T(1,128)S(1)}, s32[1,128]{1,0:T(1,128)}, u32[]{:S(2)}) %copy-start) | copy-done | bytes 536
  1.8 2.7 %shard_map.59 = bf16[128,768]{1,0:T(8,128)(2,1)S(1)} custom-call(s32[1,128]{1,0:T(1,128)S(1)} %copy-done, bf16[2048,768]{1,0:T(8,128)(2,1)} %rows_ref.1), custom_call_target="tpu_custom_call" | custom-call | bytes 1048576 | tf_op jit(solution)/shard_map/pallas_call | solution.py:224
  4.5 0.1 collective-permute-start.27
  4.6 0.5 collective-permute-start.28
  5.7 1.0 %collective-permute-done.27 = bf16[128,768]{1,0:T(8,128)(2,1)S(1)} collective-permute-done((bf16[128,768]{1,0:T(8,128)(2,1)S(1)}, bf16[128,768]{1,0:T(8,128)(2,1)S(1)}, u32[]{:S(2)}, u32[]{:S(2)}) %collective-permute-start.27) | collective-permute-done | bytes 196640 | tf_op jit(solution)/shard_map/ppermute | solution.py:184
  6.8 0.0 collective-permute-done.28
  6.8 45.5 %conditional.1 = (f32[136,768]{1,0:T(8,128)}, f32[136,768]{1,0:T(8,128)S(1)}) conditional(s32[]{:T(128)} %bitcast, (bf16[128,768]{1,0:T(8,128)(2,1)S(1)}, s32[16]{0:T(128)S(1)}, s32[16]{0:T(128)S(1)}, bf16[2048,768]{1,0:T(8,128)(2,1)S(1)}, bf16[2048,768]{1,0:T(8,128)(2,1)S(1)}) %tuple.36, (bf16[128,768]{1,0:T(8,128)(2,1)S(1)}, ...), branch_computations={%region_0.1_spmd, %region_1.2_spmd, %region_2.3_spmd} | conditional | flops 3221329920 | bytes 13492749 | solution.py:228
  6.8 3.0 %collective-permute-start.10 = (bf16[128,768]{1,0:T(8,128)(2,1)S(1)}, bf16[128,768]{1,0:T(8,128)(2,1)S(1)}, u32[]{:S(2)}, u32[]{:S(2)}) collective-permute-start(bf16[128,768]{1,0:T(8,128)(2,1)S(1)} %get-tuple-element.41.refs_2_), channel_id=1, source_target_pairs={{0,2},{1,10},{2,0},{3,8},{4,6},{5,14},{6,4},{7,12},{8,3},{9,11},{1... | collective-permute-start | bytes 589832 | tf_op jit(solution)/shard_map/cond/branch_1_fun/ppermute | solution.py:165
  9.8 0.8 %collective-permute-start.9 = (bf16[128,768]{1,0:T(8,128)(2,1)S(1)}, bf16[128,768]{1,0:T(8,128)(2,1)S(1)}, u32[]{:S(2)}, u32[]{:S(2)}) collective-permute-start(bf16[128,768]{1,0:T(8,128)(2,1)S(1)} %get-tuple-element.41.refs_2_), channel_id=1, source_target_pairs={{1,8},{3,10},{5,12},{7,14},{8,1},{10,3},{12,5},{14,7},{17,24},{19,... | collective-permute-start | bytes 589832 | tf_op jit(solution)/shard_map/cond/branch_1_fun/ppermute | solution.py:165
  10.6 4.9 %collective-permute-done.10.refs_4_ = bf16[128,768]{1,0:T(8,128)(2,1)S(1)} collective-permute-done((bf16[128,768]{1,0:T(8,128)(2,1)S(1)}, bf16[128,768]{1,0:T(8,128)(2,1)S(1)}, u32[]{:S(2)}, u32[]{:S(2)}) %collective-permute-start.10) | collective-permute-done | bytes 196640 | tf_op jit(solution)/shard_map/cond/branch_1_fun/ppermute | solution.py:165
  15.5 4.0 %branch_1_fun.3 = (bf16[136,768]{1,0:T(8,128)(2,1)S(1)}, bf16[128,768]{1,0:T(8,128)(2,1)S(1)}) custom-call(s32[16]{0:T(128)S(1)} %get-tuple-element.39.refs_0_, s32[16]{0:T(128)S(1)} %get-tuple-element.40.refs_1_, bf16[128,768]{1,0:T(8,128)(2,1)S(1)} %get-tuple-element.41.refs_2_, bf16[128,768]{1,0:T(8,128)(2,1)S(1)} %collective-permute-done.9.refs_3_, ...), custom_call_target="tpu_custom_call" | custom-call | flops 1610612736 | bytes 1048576 | tf_op jit(solution)/shard_map/cond/branch_1_fun/pallas_call | solution.py:198
  19.6 2.5 %collective-permute-start.13 = (bf16[136,768]{1,0:T(8,128)(2,1)S(1)}, bf16[136,768]{1,0:T(8,128)(2,1)S(1)}, u32[]{:S(2)}, u32[]{:S(2)}) collective-permute-start(bf16[136,768]{1,0:T(8,128)(2,1)S(1)} %get-tuple-element.45.refs_3_), channel_id=1, source_target_pairs={{0,10},{1,11},{2,8},{3,9},{4,14},{5,15},{6,12},{7,13},{8,2},{9,3},... | collective-permute-start | bytes 626696 | tf_op jit(solution)/shard_map/cond/branch_1_fun/ppermute | solution.py:179
  22.1 1.0 %collective-permute-start.12 = (bf16[136,768]{1,0:T(8,128)(2,1)S(1)}, bf16[136,768]{1,0:T(8,128)(2,1)S(1)}, u32[]{:S(2)}, u32[]{:S(2)}) collective-permute-start(bf16[136,768]{1,0:T(8,128)(2,1)S(1)} %get-tuple-element.45.refs_3_), channel_id=1, source_target_pairs={{0,8},{1,9},{2,10},{3,11},{4,12},{5,13},{6,14},{7,15},{8,0},{9,1},... | collective-permute-start | bytes 626696 | tf_op jit(solution)/shard_map/cond/branch_1_fun/ppermute | solution.py:179
  23.1 0.5 collective-permute-start.11
  23.6 4.0 %collective-permute-done.13.refs_6_ = bf16[136,768]{1,0:T(8,128)(2,1)S(1)} collective-permute-done((bf16[136,768]{1,0:T(8,128)(2,1)S(1)}, bf16[136,768]{1,0:T(8,128)(2,1)S(1)}, u32[]{:S(2)}, u32[]{:S(2)}) %collective-permute-start.13) | collective-permute-done | bytes 208928 | tf_op jit(solution)/shard_map/cond/branch_1_fun/ppermute | solution.py:179
  27.6 5.9 %collective-permute-done.12.refs_5_ = bf16[136,768]{1,0:T(8,128)(2,1)S(1)} collective-permute-done((bf16[136,768]{1,0:T(8,128)(2,1)S(1)}, bf16[136,768]{1,0:T(8,128)(2,1)S(1)}, u32[]{:S(2)}, u32[]{:S(2)}) %collective-permute-start.12) | collective-permute-done | bytes 208928 | tf_op jit(solution)/shard_map/cond/branch_1_fun/ppermute | solution.py:179
  33.5 0.0 collective-permute-done.11.refs_4_
  33.5 4.1 %branch_1_fun.4 = (bf16[136,768]{1,0:T(8,128)(2,1)S(1)}, f32[128,768]{1,0:T(8,128)S(1)}) custom-call(s32[16]{0:T(128)S(1)} %get-tuple-element.39.refs_0_, s32[16]{0:T(128)S(1)} %get-tuple-element.40.refs_1_, bf16[128,768]{1,0:T(8,128)(2,1)S(1)} %get-tuple-element.44.refs_2_, bf16[136,768]{1,0:T(8,128)(2,1)S(1)} %get-tuple-element.45.refs_3_, ...), custom_call_target="tpu_custom_call" | custom-call | flops 1610612736 | bytes 1048576 | tf_op jit(solution)/shard_map/cond/branch_1_fun/pallas_call | solution.py:205
  37.6 1.3 %collective-permute-start.16 = (bf16[136,768]{1,0:T(8,128)(2,1)S(1)}, bf16[136,768]{1,0:T(8,128)(2,1)S(1)}, u32[]{:S(2)}, u32[]{:S(2)}) collective-permute-start(bf16[136,768]{1,0:T(8,128)(2,1)S(1)} %get-tuple-element.47.refs_1_), channel_id=1, source_target_pairs={{1,11},{3,9},{5,15},{7,13},{8,2},{10,0},{12,6},{14,4},{17,27},{19,... | collective-permute-start | bytes 626696 | tf_op jit(solution)/shard_map/cond/branch_1_fun/ppermute | solution.py:179
  38.9 1.3 %collective-permute-start.15 = (bf16[136,768]{1,0:T(8,128)(2,1)S(1)}, bf16[136,768]{1,0:T(8,128)(2,1)S(1)}, u32[]{:S(2)}, u32[]{:S(2)}) collective-permute-start(bf16[136,768]{1,0:T(8,128)(2,1)S(1)} %get-tuple-element.47.refs_1_), channel_id=1, source_target_pairs={{1,9},{3,11},{5,13},{7,15},{8,0},{10,2},{12,4},{14,6},{17,25},{19,... | collective-permute-start | bytes 626696 | tf_op jit(solution)/shard_map/cond/branch_1_fun/ppermute | solution.py:179
  40.2 3.3 %collective-permute-start.14 = (bf16[136,768]{1,0:T(8,128)(2,1)S(1)}, bf16[136,768]{1,0:T(8,128)(2,1)S(1)}, u32[]{:S(2)}, u32[]{:S(2)}) collective-permute-start(bf16[136,768]{1,0:T(8,128)(2,1)S(1)} %get-tuple-element.47.refs_1_), channel_id=1, source_target_pairs={{0,2},{2,0},{4,6},{6,4},{9,11},{11,9},{13,15},{15,13},{16,18},{18,... | collective-permute-start | bytes 626696 | tf_op jit(solution)/shard_map/cond/branch_1_fun/ppermute | solution.py:179
  43.5 2.8 %collective-permute-done.16.refs_4_ = bf16[136,768]{1,0:T(8,128)(2,1)S(1)} collective-permute-done((bf16[136,768]{1,0:T(8,128)(2,1)S(1)}, bf16[136,768]{1,0:T(8,128)(2,1)S(1)}, u32[]{:S(2)}, u32[]{:S(2)}) %collective-permute-start.16) | collective-permute-done | bytes 208928 | tf_op jit(solution)/shard_map/cond/branch_1_fun/ppermute | solution.py:179
  46.3 2.1 %collective-permute-done.15.refs_3_ = bf16[136,768]{1,0:T(8,128)(2,1)S(1)} collective-permute-done((bf16[136,768]{1,0:T(8,128)(2,1)S(1)}, bf16[136,768]{1,0:T(8,128)(2,1)S(1)}, u32[]{:S(2)}, u32[]{:S(2)}) %collective-permute-start.15) | collective-permute-done | bytes 208928 | tf_op jit(solution)/shard_map/cond/branch_1_fun/ppermute | solution.py:179
  48.4 0.1 collective-permute-done.14.refs_2_
  48.5 0.1 branch_1_fun.5
  48.6 0.1 collective-permute-start.17
  48.7 1.7 %collective-permute-done.17 = f32[136,768]{1,0:T(8,128)S(1)} collective-permute-done((f32[136,768]{1,0:T(8,128)S(1)}, f32[136,768]{1,0:T(8,128)S(1)}, u32[]{:S(2)}, u32[]{:S(2)}) %collective-permute-start.17) | collective-permute-done | bytes 417824 | tf_op jit(solution)/shard_map/cond/branch_1_fun/ppermute | solution.py:184
  50.4 0.8 %broadcast_select_fusion.1 = f32[136,768]{1,0:T(8,128)} fusion(f32[136,768]{1,0:T(8,128)S(1)} %branch_1_fun.5, f32[136,768]{1,0:T(8,128)S(1)} %collective-permute-done.17, pred[]{:T(512)S(6)} %eq.7), kind=kLoop, calls=%fused_computation.1 | loop fusion | flops 104448 | bytes 1253377 | tf_op jit(solution)/shard_map/cond/branch_1_fun/jit(_where)/select_n | solution.py:217
  51.3 1.0 %copy.17 = f32[136,768]{1,0:T(8,128)S(1)} copy(f32[136,768]{1,0:T(8,128)} %broadcast_select_fusion.1) | data formatting | bytes 835584 | tf_op jit(solution)/shard_map/cond
  52.3 0.5 slice.19
  52.8 0.8 %slice_bitcast_fusion = f32[1,128,768]{2,1,0:T(8,128)} fusion(f32[136,768]{1,0:T(8,128)S(1)} %get-tuple-element.60), kind=kLoop, calls=%fused_computation.3 | loop fusion | bytes 786432 | tf_op jit(solution)/shard_map/cond/branch_0_fun/broadcast_in_dim | solution.py:218
  (8 shorter events, 0.1 us)
Async XLA Ops:
  0.6 6.2 %collective-permute-start.29 = (bf16[2048,768]{1,0:T(8,128)(2,1)}, bf16[2048,768]{1,0:T(8,128)(2,1)S(1)}, u32[]{:S(2)}, u32[]{:S(2)}) collective-permute-start(bf16[2048,768]{1,0:T(8,128)(2,1)} %rows_ref.1), channel_id=1, source_target_pairs={{0,1},{1,0},{2,3},{3,2},{4,5},{5,4},{6,7},{7,6},{8,9},{9,8},{10,11... | collective-permute-start | bytes 9437192 | tf_op jit(solution)/shard_map/ppermute | solution.py:184
  1.1 0.7 %copy-start = (s32[1,128]{1,0:T(1,128)S(1)}, s32[1,128]{1,0:T(1,128)}, u32[]{:S(2)}) copy-start(s32[1,128]{1,0:T(1,128)} %index_ref.1) | copy-start | bytes 1540
  1.8 2.8 %copy-start.2 = (s32[16]{0:T(128)S(1)}, s32[16]{0:T(128)}, u32[]{:S(2)}) copy-start(s32[16]{0:T(128)} %param.8) | copy-start | bytes 196
  1.8 5.0 %copy-start.1 = (bf16[2048,768]{1,0:T(8,128)(2,1)S(1)}, bf16[2048,768]{1,0:T(8,128)(2,1)}, u32[]{:S(2)}) copy-start(bf16[2048,768]{1,0:T(8,128)(2,1)} %rows_ref.1) | copy-start | bytes 9437188
  4.5 2.2 %collective-permute-start.27 = (bf16[128,768]{1,0:T(8,128)(2,1)S(1)}, bf16[128,768]{1,0:T(8,128)(2,1)S(1)}, u32[]{:S(2)}, u32[]{:S(2)}) collective-permute-start(bf16[128,768]{1,0:T(8,128)(2,1)S(1)} %shard_map.59), channel_id=1, source_target_pairs={{0,1},{1,0},{2,3},{3,2},{4,5},{5,4},{6,7},{7,6},{8,9},{9,8},{10,11... | collective-permute-start | bytes 589832 | tf_op jit(solution)/shard_map/ppermute | solution.py:184
  4.6 2.1 %collective-permute-start.28 = (s32[16]{0:T(128)S(1)}, s32[16]{0:T(128)S(1)}, u32[]{:S(2)}, u32[]{:S(2)}) collective-permute-start(s32[16]{0:T(128)S(1)} %copy-done.2), channel_id=1, source_target_pairs={{0,1},{1,0},{2,3},{3,2},{4,5},{5,4},{6,7},{7,6},{8,9},{9,8},{10,11... | collective-permute-start | bytes 200 | tf_op jit(solution)/shard_map/ppermute | solution.py:184
  6.8 8.7 %collective-permute-start.10 = (bf16[128,768]{1,0:T(8,128)(2,1)S(1)}, bf16[128,768]{1,0:T(8,128)(2,1)S(1)}, u32[]{:S(2)}, u32[]{:S(2)}) collective-permute-start(bf16[128,768]{1,0:T(8,128)(2,1)S(1)} %get-tuple-element.41.refs_2_), channel_id=1, source_target_pairs={{0,2},{1,10},{2,0},{3,8},{4,6},{5,14},{6,4},{7,12},{8,3},{9,11},{1... | collective-permute-start | bytes 589832 | tf_op jit(solution)/shard_map/cond/branch_1_fun/ppermute | solution.py:165
  9.8 5.8 %collective-permute-start.9 = (bf16[128,768]{1,0:T(8,128)(2,1)S(1)}, bf16[128,768]{1,0:T(8,128)(2,1)S(1)}, u32[]{:S(2)}, u32[]{:S(2)}) collective-permute-start(bf16[128,768]{1,0:T(8,128)(2,1)S(1)} %get-tuple-element.41.refs_2_), channel_id=1, source_target_pairs={{1,8},{3,10},{5,12},{7,14},{8,1},{10,3},{12,5},{14,7},{17,24},{19,... | collective-permute-start | bytes 589832 | tf_op jit(solution)/shard_map/cond/branch_1_fun/ppermute | solution.py:165
  19.6 8.1 %collective-permute-start.13 = (bf16[136,768]{1,0:T(8,128)(2,1)S(1)}, bf16[136,768]{1,0:T(8,128)(2,1)S(1)}, u32[]{:S(2)}, u32[]{:S(2)}) collective-permute-start(bf16[136,768]{1,0:T(8,128)(2,1)S(1)} %get-tuple-element.45.refs_3_), channel_id=1, source_target_pairs={{0,10},{1,11},{2,8},{3,9},{4,14},{5,15},{6,12},{7,13},{8,2},{9,3},... | collective-permute-start | bytes 626696 | tf_op jit(solution)/shard_map/cond/branch_1_fun/ppermute | solution.py:179
  22.1 11.4 %collective-permute-start.12 = (bf16[136,768]{1,0:T(8,128)(2,1)S(1)}, bf16[136,768]{1,0:T(8,128)(2,1)S(1)}, u32[]{:S(2)}, u32[]{:S(2)}) collective-permute-start(bf16[136,768]{1,0:T(8,128)(2,1)S(1)} %get-tuple-element.45.refs_3_), channel_id=1, source_target_pairs={{0,8},{1,9},{2,10},{3,11},{4,12},{5,13},{6,14},{7,15},{8,0},{9,1},... | collective-permute-start | bytes 626696 | tf_op jit(solution)/shard_map/cond/branch_1_fun/ppermute | solution.py:179
  23.1 10.4 %collective-permute-start.11 = (bf16[136,768]{1,0:T(8,128)(2,1)S(1)}, bf16[136,768]{1,0:T(8,128)(2,1)S(1)}, u32[]{:S(2)}, u32[]{:S(2)}) collective-permute-start(bf16[136,768]{1,0:T(8,128)(2,1)S(1)} %get-tuple-element.45.refs_3_), channel_id=1, source_target_pairs={{0,2},{1,3},{2,0},{3,1},{4,6},{5,7},{6,4},{7,5},{8,10},{9,11},{10,... | collective-permute-start | bytes 626696 | tf_op jit(solution)/shard_map/cond/branch_1_fun/ppermute | solution.py:179
  37.6 8.6 %collective-permute-start.16 = (bf16[136,768]{1,0:T(8,128)(2,1)S(1)}, bf16[136,768]{1,0:T(8,128)(2,1)S(1)}, u32[]{:S(2)}, u32[]{:S(2)}) collective-permute-start(bf16[136,768]{1,0:T(8,128)(2,1)S(1)} %get-tuple-element.47.refs_1_), channel_id=1, source_target_pairs={{1,11},{3,9},{5,15},{7,13},{8,2},{10,0},{12,6},{14,4},{17,27},{19,... | collective-permute-start | bytes 626696 | tf_op jit(solution)/shard_map/cond/branch_1_fun/ppermute | solution.py:179
  38.9 9.4 %collective-permute-start.15 = (bf16[136,768]{1,0:T(8,128)(2,1)S(1)}, bf16[136,768]{1,0:T(8,128)(2,1)S(1)}, u32[]{:S(2)}, u32[]{:S(2)}) collective-permute-start(bf16[136,768]{1,0:T(8,128)(2,1)S(1)} %get-tuple-element.47.refs_1_), channel_id=1, source_target_pairs={{1,9},{3,11},{5,13},{7,15},{8,0},{10,2},{12,4},{14,6},{17,25},{19,... | collective-permute-start | bytes 626696 | tf_op jit(solution)/shard_map/cond/branch_1_fun/ppermute | solution.py:179
  40.2 8.2 %collective-permute-start.14 = (bf16[136,768]{1,0:T(8,128)(2,1)S(1)}, bf16[136,768]{1,0:T(8,128)(2,1)S(1)}, u32[]{:S(2)}, u32[]{:S(2)}) collective-permute-start(bf16[136,768]{1,0:T(8,128)(2,1)S(1)} %get-tuple-element.47.refs_1_), channel_id=1, source_target_pairs={{0,2},{2,0},{4,6},{6,4},{9,11},{11,9},{13,15},{15,13},{16,18},{18,... | collective-permute-start | bytes 626696 | tf_op jit(solution)/shard_map/cond/branch_1_fun/ppermute | solution.py:179
  48.6 1.8 %collective-permute-start.17 = (f32[136,768]{1,0:T(8,128)S(1)}, f32[136,768]{1,0:T(8,128)S(1)}, u32[]{:S(2)}, u32[]{:S(2)}) collective-permute-start(f32[136,768]{1,0:T(8,128)S(1)} %branch_1_fun.5), channel_id=1, source_target_pairs={{0,1},{1,0},{2,3},{3,2},{4,5},{5,4},{6,7},{7,6},{8,9},{9,8},{10,11... | collective-permute-start | bytes 1253384 | tf_op jit(solution)/shard_map/cond/branch_1_fun/ppermute | solution.py:184
